TPU v7x, 32 devices: a whole 2x2x4 slice. The times are simulated.
32 devices in a mesh: region: 8 (over z, y), member: 4 (over x, core).
Axes of the slice: x: 2, y: 2, z: 4, core: 2. Of those that a mesh axis runs over, the one named last changes fastest.
Arguments:
- ensemble: bfloat16 [256, 16384], P('member', 'region'), may hold values from -6 to 6
- reports: float32 [8, 1024], P('region'), may hold values from -6 to 6
- report_count: int32 [8], P('region'), may hold values from 128 to 1024, as said below
- report_cell: int32 [8, 1024], P('region'), may hold values from 0 to 16383, as said below
- report_weight: float32 [8, 16, 1024], P('region', 'member'), may hold values from 0.001 to 1
- blending: float32 [4, 16384], P(None, ('region', 'member')), may hold values from 0.02 to 1
Outputs:
- analysis: bfloat16 [16384, 256], P(('region', 'member'))
Inputs may be any that keep to these rules, and one draw needn't show every extreme that they name: `report_count`: the largest value 1024 is reached by some region in every draw. `report_cell`: every cell lies in the slot's own region, or in the first 128 cells of one of at most two other regions chosen for that region.
All inputs are finite; a program needn't handle non-finite values.
Results may differ from a plain program's by a relative error of at most 0.0055.
Values may be sent and summed in bfloat16 or wider, within the bound.
No kernel may reach another device: no remote copies, remote signals or barrier semaphores. Data moves between devices by JAX's collectives and lax.ppermute only.
A program may use at most 64 MiB of HBM per device.

v0:
```python
import jax
import jax.numpy as jnp
from jax import lax
from jax.sharding import PartitionSpec as P

MARGIN = 128
SWEEPS = 4
highest = lax.Precision.HIGHEST


def extended(block, sides, width):
    for axis, dim in sides:
        count = lax.axis_size(axis)
        forward = [(i, i + 1) for i in range(count - 1)]
        backward = [(target, source) for source, target in forward]
        low = lax.ppermute(
            lax.slice_in_dim(block, block.shape[dim] - width, None, axis=dim), axis, forward
        )
        high = lax.ppermute(lax.slice_in_dim(block, 0, width, axis=dim), axis, backward)
        block = jnp.concatenate([low, block, high], axis=dim)
    return block


def make_transform(products, forcing, members):
    identity = jnp.eye(members, dtype=jnp.float32)
    precision_mat = (members - 1.0) * identity[None] + products
    frobenius = jnp.sqrt(jnp.sum(precision_mat * precision_mat, axis=(1, 2)))
    current = precision_mat / frobenius[:, None, None]
    root_iter = jnp.broadcast_to(identity, current.shape)
    for iteration in range(SWEEPS):
        middle = 1.5 * identity[None] - 0.5 * jnp.einsum(
            "aij,ajk->aik", root_iter, current, precision=highest
        )
        current = jnp.einsum("aij,ajk->aik", current, middle, precision=highest)
        root_iter = jnp.einsum("aij,ajk->aik", middle, root_iter, precision=highest)
    inverse_root = root_iter / jnp.sqrt(frobenius)[:, None, None]
    inner_step = jnp.einsum("aij,aj->ai", inverse_root, forcing, precision=highest)
    mean_weights = jnp.einsum("aij,aj->ai", inverse_root, inner_step, precision=highest)
    return (mean_weights[:, :, None] + jnp.sqrt(members - 1.0) * inverse_root).astype(jnp.bfloat16)


def corner_layout(band_index, points_here, row_count):
    group_index = jnp.arange(4 * points_here, dtype=jnp.int32)
    upper_half = group_index // (2 * points_here)
    column_block = group_index // 2 % points_here
    right_half = group_index % 2
    row_base = jnp.clip(band_index - 1 + upper_half, 0, row_count - 2)
    col_base = jnp.clip(column_block - 1 + right_half, 0, points_here - 2)
    return (row_base, col_base)


def per_device(ensemble, reports, report_count, report_cell, report_weight, blending):
    local_members, cell_count = ensemble.shape
    groups = lax.axis_size("member")
    members = local_members * groups
    region = lax.axis_index("region")
    member = lax.axis_index("member")
    targets = report_cell[0]
    holder = targets // cell_count
    within = targets % cell_count
    is_local = holder == region
    local_values = jnp.take(ensemble, jnp.where(is_local, within, 0), axis=1).astype(jnp.float32)
    border = ensemble[:, :MARGIN]
    border_index = holder * MARGIN + jnp.minimum(within, MARGIN - 1)
    pieces = lax.all_gather(border, "region", axis=1, tiled=True)
    extent = pieces.shape[1]
    inside = (border_index >= 0) & (border_index < extent) & jnp.logical_not(is_local)
    picked = jnp.take(pieces, jnp.clip(border_index, 0, extent - 1), axis=1).astype(jnp.float32)
    remote = jnp.where(inside[None, :], picked, 0.0)
    at_reports = jnp.where(is_local[None, :], local_values, remote)
    report_mean = lax.psum(jnp.sum(at_reports, axis=0), "member") / members
    local_pert = (at_reports - report_mean[None, :]).astype(jnp.bfloat16)
    report_pert = lax.all_gather(local_pert, "member", axis=0, tiled=True)
    active = (jnp.arange(report_pert.shape[1]) < report_count[0]).astype(jnp.float32)
    weights = report_weight[0] * active[None, :]
    weighted = (report_pert[None, :, :] * weights[:, None, :]).astype(jnp.bfloat16)
    departure = (weights * (reports[0] - report_mean)[None, :]).astype(jnp.bfloat16)
    products = jnp.einsum("ako,jo->akj", weighted, report_pert, preferred_element_type=jnp.float32)
    forcing = jnp.einsum("ao,ko->ak", departure, report_pert, preferred_element_type=jnp.float32)
    transform = make_transform(products, forcing, members)
    points_here = transform.shape[0]
    groups_band = 4 * points_here
    slab_cells = cell_count // groups
    group_cells = slab_cells // groups_band
    mixing = blending / jnp.sum(blending, axis=0, keepdims=True)
    columns = lax.all_to_all(ensemble, "member", split_axis=1, concat_axis=0, tiled=True)
    cell_mean = jnp.sum(columns, axis=0, dtype=jnp.float32) / members
    anomaly = (columns - cell_mean[None, :]).astype(jnp.bfloat16)
    anomaly_view = anomaly.reshape(members, groups_band, group_cells)
    mix_view = mixing.reshape(4, groups_band, group_cells)
    neighbours = extended(transform[None], (("member", 0),), 1)
    stacked = neighbours.reshape(3 * points_here, members, members)
    row_base, col_base = corner_layout(member, points_here, groups)
    running = jnp.zeros((groups_band, group_cells, members), jnp.float32)
    for corner in range(4):
        row_step = corner // 2
        col_step = corner % 2
        chosen_index = (row_base + row_step - (member - 1)) * points_here + col_base + col_step
        chosen = jnp.take(stacked, chosen_index, axis=0)
        spread = jnp.einsum(
            "kgc,gkj->gcj", anomaly_view, chosen, preferred_element_type=jnp.float32
        )
        running = running + mix_view[corner][:, :, None] * spread
    blended = running.reshape(slab_cells, members)
    return (cell_mean[:, None] + blended).astype(jnp.bfloat16)


def solution(mesh):
    return jax.shard_map(
        per_device,
        mesh=mesh,
        in_specs=(
            P("member", "region"),
            P("region", None),
            P("region"),
            P("region", None),
            P("region", "member", None),
            P(None, ("region", "member")),
        ),
        out_specs=P(("region", "member"), None),
        check_vma=False,
    )
```

profile of v0, /device:TPU:0, one launch (start us, length us, event | category | flops | bytes accessed | tf_op | source)
XLA Modules:
  0.0 104.7 jit_solution(4873198254214473473)
XLA Ops:
  0.0 0.8 compare_select_fusion
  1.6 1.2 %copy.24 = bf16[64,2048]{0,1:T(8,128)(2,1)S(1)} copy(bf16[64,2048]{1,0:T(8,128)(2,1)} %param.8) | data formatting | bytes 524288 | tf_op args[0]
  2.9 3.2 %gather_fusion = bf16[1024,64]{1,0:T(8,128)(2,1)S(1)} fusion(bf16[64,2048]{0,1:T(8,128)(2,1)S(1)} %copy.24, s32[1024]{0:T(1024)S(1)} %broadcast_clamp_fusion.1), kind=kCustom, calls=%fused_computation.4 | custom fusion | bytes 266240 | tf_op jit(solution)/shard_map/jit(_take)/gather | solution.py:62
  6.3 32.6 %all_gather.6 = bf16[64,1024]{0,1:T(8,128)(2,1)S(1)} all-gather(bf16[64,128]{0,1:T(8,128)(2,1)S(1)} %slice.37), channel_id=1, replica_groups=mesh['region'=8,'member'=4] {'region'}, dimensions={1}, use_global_device_ids=true | all-gather | bytes 147456 | tf_op jit(solution)/shard_map/all_gather | solution.py:65
  38.9 3.2 %gather_fusion.1 = bf16[1024,64]{1,0:T(8,128)(2,1)S(1)} fusion(bf16[64,1024]{0,1:T(8,128)(2,1)S(1)} %all_gather.6, s32[1024]{0:T(1024)S(1)} %broadcast_clamp_fusion), kind=kCustom, calls=%fused_computation.5 | custom fusion | bytes 266240 | tf_op jit(solution)/shard_map/jit(_take)/gather | solution.py:68
  42.3 5.7 %psum.7 = f32[1024]{0:T(1024)S(1)} all-reduce(f32[1024]{0:T(1024)S(1)} %fusion.54), channel_id=1, replica_groups=mesh['region'=8,'member'=4] {'member'}, use_global_device_ids=true, to_apply=%region_3.4 | all-reduce | flops 1024 | bytes 8192 | tf_op jit(solution)/shard_map/psum | solution.py:71
  48.1 7.4 %all_gather.7 = bf16[256,1024]{1,0:T(8,128)(2,1)S(1)} all-gather(bf16[64,1024]{1,0:T(8,128)(2,1)S(1)} %fusion.56), channel_id=1, replica_groups=mesh['region'=8,'member'=4] {'member'}, dimensions={0}, use_global_device_ids=true | all-gather | bytes 655360 | tf_op jit(solution)/shard_map/all_gather | solution.py:73
  56.3 0.9 multiply_reduce_fusion
  57.2 1.2 %fusion.19 = f32[4,256,256]{2,1,0:T(8,128)S(1)} fusion(f32[256,256]{1,0:T(8,128)S(1)} %fusion.52, f32[256,256]{1,0:T(8,128)S(1)} %fusion.53, f32[4,256,256]{2,1,0:T(8,128)S(1)} %get-tuple-element.24, f32[4]{0:T(128)S(1)} %get-tuple-element.22), kind=kOutput, calls=%fused_computation.32 | convolution fusion | flops 806092800 | bytes 2621456 | tf_op jit(solution)/shard_map/aij,ajk->aik/dot_general | solution.py:31
  58.4 1.2 %fusion.55 = f32[4,256,256]{2,1,0:T(8,128)S(1)} fusion(f32[4,256,256]{2,1,0:T(8,128)S(1)} %fusion.19, f32[4,256,256]{2,1,0:T(8,128)S(1)} %get-tuple-element.24, f32[4]{0:T(128)S(1)} %get-tuple-element.22), kind=kOutput, calls=%fused_computation.66 | convolution fusion | flops 805568512 | bytes 3145744 | tf_op jit(solution)/shard_map/aij,ajk->aik/dot_general | solution.py:34
  59.6 1.1 %fusion.48 = f32[4,256,256]{2,1,0:T(8,128)S(1)} fusion(f32[4,256,256]{2,1,0:T(8,128)S(1)} %fusion.19, f32[256,256]{1,0:T(8,128)S(1)} %fusion.52), kind=kOutput, calls=%fused_computation.54 | convolution fusion | flops 805306368 | bytes 2359296 | tf_op jit(solution)/shard_map/aij,ajk->aik/dot_general | solution.py:35
  60.7 1.2 %fusion.18 = f32[4,256,256]{2,1,0:T(8,128)S(1)} fusion(f32[4,256,256]{2,1,0:T(8,128)S(1)} %fusion.48, f32[4,256,256]{2,1,0:T(8,128)S(1)} %fusion.55, f32[256,256]{1,0:T(8,128)S(1)} %fusion.53), kind=kOutput, calls=%fused_computation.30 | convolution fusion | flops 805830656 | bytes 3407872 | tf_op jit(solution)/shard_map/aij,ajk->aik/dot_general | solution.py:31
  61.9 1.1 %fusion.79 = f32[4,256,256]{2,1,0:T(8,128)S(1)} fusion(f32[4,256,256]{2,1,0:T(8,128)S(1)} %fusion.55, f32[4,256,256]{2,1,0:T(8,128)S(1)} %fusion.18), kind=kOutput, calls=%fused_computation.158 | convolution fusion | flops 805306368 | bytes 3145728 | tf_op jit(solution)/shard_map/aij,ajk->aik/dot_general | solution.py:34
  63.0 1.1 %fusion.78 = f32[4,256,256]{2,1,0:T(8,128)S(1)} fusion(f32[4,256,256]{2,1,0:T(8,128)S(1)} %fusion.18, f32[4,256,256]{2,1,0:T(8,128)S(1)} %fusion.48), kind=kOutput, calls=%fused_computation.157 | convolution fusion | flops 805306368 | bytes 3145728 | tf_op jit(solution)/shard_map/aij,ajk->aik/dot_general | solution.py:35
  64.2 1.2 %fusion.17 = f32[4,256,256]{2,1,0:T(8,128)S(1)} fusion(f32[4,256,256]{2,1,0:T(8,128)S(1)} %fusion.78, f32[4,256,256]{2,1,0:T(8,128)S(1)} %fusion.79, f32[256,256]{1,0:T(8,128)S(1)} %fusion.53), kind=kOutput, calls=%fused_computation.28 | convolution fusion | flops 805830656 | bytes 3407872 | tf_op jit(solution)/shard_map/aij,ajk->aik/dot_general | solution.py:31
  65.4 1.1 %fusion.81 = f32[4,256,256]{2,1,0:T(8,128)S(1)} fusion(f32[4,256,256]{2,1,0:T(8,128)S(1)} %fusion.79, f32[4,256,256]{2,1,0:T(8,128)S(1)} %fusion.17), kind=kOutput, calls=%fused_computation.160 | convolution fusion | flops 805306368 | bytes 3145728 | tf_op jit(solution)/shard_map/aij,ajk->aik/dot_general | solution.py:34
  66.5 1.1 %fusion.80 = f32[4,256,256]{2,1,0:T(8,128)S(1)} fusion(f32[4,256,256]{2,1,0:T(8,128)S(1)} %fusion.17, f32[4,256,256]{2,1,0:T(8,128)S(1)} %fusion.78), kind=kOutput, calls=%fused_computation.159 | convolution fusion | flops 805306368 | bytes 3145728 | tf_op jit(solution)/shard_map/aij,ajk->aik/dot_general | solution.py:35
  67.9 1.4 %fusion.16 = f32[4,256,256]{2,1,0:T(8,128)S(1)} fusion(f32[4,256,256]{2,1,0:T(8,128)S(1)} %fusion.80, f32[4,256,256]{2,1,0:T(8,128)S(1)} %fusion.81, f32[256,256]{1,0:T(8,128)S(1)} %fusion.53), kind=kOutput, calls=%fused_computation.26 | convolution fusion | flops 805830656 | bytes 3407872 | tf_op jit(solution)/shard_map/aij,ajk->aik/dot_general | solution.py:31
  69.3 1.1 %convolution_divide_fusion = f32[4,256,256]{2,1,0:T(8,128)S(1)} fusion(f32[4,256,256]{2,1,0:T(8,128)S(1)} %fusion.16, f32[4,256,256]{2,1,0:T(8,128)S(1)} %fusion.80, f32[4]{0:T(128)S(1)} %get-tuple-element.21), kind=kOutput, calls=%fused_computation.24 | convolution fusion | flops 805568512 | bytes 3145744 | tf_op jit(solution)/shard_map/aij,ajk->aik/dot_general | solution.py:35
  70.5 1.0 fusion.62
  71.5 1.0 fusion.60
  72.7 2.3 %collective-permute-start = (bf16[1,4,256,256]{3,2,1,0:T(8,128)(2,1)S(1)}, bf16[1,4,256,256]{3,2,1,0:T(8,128)(2,1)S(1)}, u32[]{:S(2)}, u32[]{:S(2)}) collective-permute-start(bf16[1,4,256,256]{3,2,1,0:T(8,128)(2,1)S(1)} %fusion.45), channel_id=1, source_target_pairs={{0,1},{1,2},{2,3},{4,5},{5,6},{6,7},{8,9},{9,10},{10,11},{12,13},{... | collective-permute-start | bytes 1572872 | tf_op jit(solution)/shard_map/ppermute | solution.py:16
  75.0 1.3 %collective-permute-start.1 = (bf16[1,4,256,256]{3,2,1,0:T(8,128)(2,1)S(1)}, bf16[1,4,256,256]{3,2,1,0:T(8,128)(2,1)S(1)}, u32[]{:S(2)}, u32[]{:S(2)}) collective-permute-start(bf16[1,4,256,256]{3,2,1,0:T(8,128)(2,1)S(1)} %fusion.45), channel_id=1, source_target_pairs={{1,0},{2,1},{3,2},{5,4},{6,5},{7,6},{9,8},{10,9},{11,10},{13,12},{... | collective-permute-start | bytes 1572872 | tf_op jit(solution)/shard_map/ppermute | solution.py:19
  77.0 4.1 %all-to-all-start = ((bf16[64,4,512]{2,0,1:T(8,128)(2,1)}), bf16[64,4,512]{2,0,1:T(8,128)(2,1)S(1)}, u32[]{:S(2)}, u32[]{:S(2)}) async-start(bf16[64,4,512]{2,0,1:T(8,128)(2,1)} %bitcast.73), calls=%async_computation | async-start | bytes 524288 | tf_op jit(solution)/shard_map/all_to_all | solution.py:86
  81.7 7.4 %all-to-all-done = bf16[64,4,512]{2,0,1:T(8,128)(2,1)S(1)} async-done(((bf16[64,4,512]{2,0,1:T(8,128)(2,1)}), bf16[64,4,512]{2,0,1:T(8,128)(2,1)S(1)}, u32[]{:S(2)}, u32[]{:S(2)}) %all-to-all-start) | async-done | bytes 262176 | tf_op jit(solution)/shard_map/all_to_all | solution.py:86
  90.7 2.0 %gather_fusion.3 = bf16[16,256,256]{2,1,0:T(8,128)(2,1)} fusion(bf16[12,256,256]{2,1,0:T(8,128)(2,1)S(1)} %bitcast.77, s32[1024]{0:T(1024)S(1)} %pad_clamp_fusion.2), kind=kCustom, calls=%fused_computation.1.clone | custom fusion | bytes 4194368 | tf_op jit(solution)/shard_map/jit(_take)/gather | solution.py:99
  92.7 2.0 %gather_fusion.4 = bf16[16,256,256]{2,1,0:T(8,128)(2,1)} fusion(bf16[12,256,256]{2,1,0:T(8,128)(2,1)S(1)} %bitcast.78, s32[1024]{0:T(1024)S(1)} %pad_clamp_fusion.1), kind=kCustom, calls=%fused_computation.2.clone | custom fusion | bytes 4194368 | tf_op jit(solution)/shard_map/jit(_take)/gather | solution.py:99
  94.7 2.0 %gather_fusion.5 = bf16[16,256,256]{2,1,0:T(8,128)(2,1)} fusion(bf16[12,256,256]{2,1,0:T(8,128)(2,1)S(1)} %bitcast.79, s32[1024]{0:T(1024)S(1)} %pad_clamp_fusion), kind=kCustom, calls=%fused_computation.3.clone | custom fusion | bytes 4194368 | tf_op jit(solution)/shard_map/jit(_take)/gather | solution.py:99
  96.7 2.0 %gather_fusion.2 = bf16[16,256,256]{2,1,0:T(8,128)(2,1)} fusion(bf16[12,256,256]{2,1,0:T(8,128)(2,1)S(1)} %bitcast.80, s32[1024]{0:T(1024)S(1)} %pad_clamp_fusion.3), kind=kCustom, calls=%fused_computation.clone | custom fusion | bytes 4194368 | tf_op jit(solution)/shard_map/jit(_take)/gather | solution.py:99
  98.7 2.3 %fusion.29 = f32[16,32,256]{2,1,0:T(8,128)S(1)} fusion(bf16[256,16,32]{0,2,1:T(8,128)(2,1)S(1)} %subtract_convert_fusion, bf16[16,256,256]{2,1,0:T(8,128)(2,1)} %gather_fusion.3, pred[16]{0:T(512)(128)(4,1)S(1)} %compare_and_fusion.4, f32[16,32]{1,0:T(8,128)S(1)} %mul.175), kind=kOutput, calls=%fused_computation.36 | convolution fusion | flops 68288512 | bytes 2885648 | tf_op jit(solution)/shard_map/kgc,gkj->gcj/dot_general | solution.py:100
  101.5 1.0 copy-done.1
  103.9 0.8 fusion.46
  (68 shorter events, 6.4 us)
Async XLA Ops:
  0.0 6.2 %copy-start.4 = (s32[1,1024]{1,0:T(1,128)S(1)}, s32[1,1024]{1,0:T(1,128)}, u32[]{:S(2)}) copy-start(s32[1,1024]{1,0:T(1,128)} %param.11) | copy-start | bytes 12292
  2.9 45.1 %copy-start.7 = (f32[1,1024]{1,0:T(1,128)S(1)}, f32[1,1024]{1,0:T(1,128)}, u32[]{:S(2)}) copy-start(f32[1,1024]{1,0:T(1,128)} %param.9) | copy-start | bytes 12292
  38.9 17.5 %copy-start.6 = (f32[1,4,1024]{2,1,0:T(4,128)S(1)}, f32[1,4,1024]{2,1,0:T(4,128)}, u32[]{:S(2)}) copy-start(f32[1,4,1024]{2,1,0:T(4,128)} %param.12) | copy-start | bytes 49156
  70.5 5.8 %copy-start.3 = (bf16[64,2048]{1,0:T(8,128)(2,1)S(1)}, bf16[64,2048]{1,0:T(8,128)(2,1)}, u32[]{:S(2)}) copy-start(bf16[64,2048]{1,0:T(8,128)(2,1)} %param.8) | copy-start | bytes 786436
  71.5 9.8 %copy-start.5 = (f32[4,512]{1,0:T(4,128)S(1)}, f32[4,512]{1,0:T(4,128)}, u32[]{:S(2)}) copy-start(f32[4,512]{1,0:T(4,128)} %param.13) | copy-start | bytes 24580
  72.7 17.8 %collective-permute-start = (bf16[1,4,256,256]{3,2,1,0:T(8,128)(2,1)S(1)}, bf16[1,4,256,256]{3,2,1,0:T(8,128)(2,1)S(1)}, u32[]{:S(2)}, u32[]{:S(2)}) collective-permute-start(bf16[1,4,256,256]{3,2,1,0:T(8,128)(2,1)S(1)} %fusion.45), channel_id=1, source_target_pairs={{0,1},{1,2},{2,3},{4,5},{5,6},{6,7},{8,9},{9,10},{10,11},{12,13},{... | collective-permute-start | bytes 1572872 | tf_op jit(solution)/shard_map/ppermute | solution.py:16
  75.0 15.5 %collective-permute-start.1 = (bf16[1,4,256,256]{3,2,1,0:T(8,128)(2,1)S(1)}, bf16[1,4,256,256]{3,2,1,0:T(8,128)(2,1)S(1)}, u32[]{:S(2)}, u32[]{:S(2)}) collective-permute-start(bf16[1,4,256,256]{3,2,1,0:T(8,128)(2,1)S(1)} %fusion.45), channel_id=1, source_target_pairs={{1,0},{2,1},{3,2},{5,4},{6,5},{7,6},{9,8},{10,9},{11,10},{13,12},{... | collective-permute-start | bytes 1572872 | tf_op jit(solution)/shard_map/ppermute | solution.py:19
  77.0 12.1 %all-to-all-start = ((bf16[64,4,512]{2,0,1:T(8,128)(2,1)}), bf16[64,4,512]{2,0,1:T(8,128)(2,1)S(1)}, u32[]{:S(2)}, u32[]{:S(2)}) async-start(bf16[64,4,512]{2,0,1:T(8,128)(2,1)} %bitcast.73), calls=%async_computation | async-start | bytes 524288 | tf_op jit(solution)/shard_map/all_to_all | solution.py:86
  98.7 2.3 %copy-start.2 = (bf16[16,256,256]{2,1,0:T(8,128)(2,1)S(1)}, bf16[16,256,256]{2,1,0:T(8,128)(2,1)}, u32[]{:S(2)}) copy-start(bf16[16,256,256]{2,1,0:T(8,128)(2,1)} %gather_fusion.4) | copy-start | bytes 6291460
  101.0 1.6 %copy-start.1 = (bf16[16,256,256]{2,1,0:T(8,128)(2,1)S(1)}, bf16[16,256,256]{2,1,0:T(8,128)(2,1)}, u32[]{:S(2)}) copy-start(bf16[16,256,256]{2,1,0:T(8,128)(2,1)} %gather_fusion.5) | copy-start | bytes 6291460
  101.5 1.8 %copy-start = (bf16[16,256,256]{2,1,0:T(8,128)(2,1)S(1)}, bf16[16,256,256]{2,1,0:T(8,128)(2,1)}, u32[]{:S(2)}) copy-start(bf16[16,256,256]{2,1,0:T(8,128)(2,1)} %gather_fusion.2) | copy-start | bytes 6291460
where the time goes:
time: 105 us
  blocking collectives  45.6 us (43%)
  matrix products  19.8 us (19%)
  local copies, waits for them, and re-layouts  19.4 us (18%)
  starting transfers between devices  7.71 us (7%)
  waiting for transfers between devices  7.42 us (7%)
  other arithmetic  3.57 us (3%)
  between operations  1.12 us (1%)
    all_gather x1, blocking collectives, per_device(): pieces = lax.all_gather(border, 'region', axis=1, tiled=True)  32.6 us
    gather x4, local copies, waits for them, and re-layouts, per_device(): chosen = jnp.take(stacked, chosen_index, axis=0)  8.04 us
    all_to_all x1, waiting for transfers between devices, per_device(): lax.all_to_all(ensemble, 'member', split_axis=1, concat_axis=0, tiled=True)  7.41 us
    all_gather x1, blocking collectives, per_device(): report_pert = lax.all_gather(local_pert, 'member', axis=0, tiled=True)  7.41 us
    psum x1, blocking collectives, per_device(): report_mean = lax.psum(jnp.sum(at_reports, axis=0), 'member') / members  5.67 us
    dot_general x4, matrix products, make_transform(): jnp.einsum('aij,ajk->aik', root_iter, current, precision=highest)  4.92 us
    dot_general x4, matrix products, make_transform(): root_iter = jnp.einsum('aij,ajk->aik', middle, root_iter, precision=highest)  4.53 us
    all_to_all x1, starting transfers between devices, per_device(): lax.all_to_all(ensemble, 'member', split_axis=1, concat_axis=0, tiled=True)  4.14 us
  transfers between devices with their start and end apart: 3, of which 1 were waited for; matrix products, arithmetic and copies ran while one was open for 2% of the time, Pallas kernels for 0%

commit v1 on v0

--- a/solution.py
+++ b/solution.py
@@ -6,6 +6,18 @@
 MARGIN = 128
 SWEEPS = 4
 highest = lax.Precision.HIGHEST
+
+
+def doubled_up(x, axis, dim):
+    ways, here = (lax.axis_size(axis), lax.axis_index(axis))
+    grown, reach = (x, 1)
+    while reach < ways:
+        theirs = lax.ppermute(grown, axis, [(d, d ^ reach) for d in range(ways)])
+        mine_first = jnp.concatenate([grown, theirs], axis=dim)
+        theirs_first = jnp.concatenate([theirs, grown], axis=dim)
+        grown = jnp.where(here & reach == 0, mine_first, theirs_first)
+        reach = 2 * reach
+    return grown
 
 
 def extended(block, sides, width):
@@ -70,7 +82,7 @@
     at_reports = jnp.where(is_local[None, :], local_values, remote)
     report_mean = lax.psum(jnp.sum(at_reports, axis=0), "member") / members
     local_pert = (at_reports - report_mean[None, :]).astype(jnp.bfloat16)
-    report_pert = lax.all_gather(local_pert, "member", axis=0, tiled=True)
+    report_pert = doubled_up(local_pert, "member", 0)
     active = (jnp.arange(report_pert.shape[1]) < report_count[0]).astype(jnp.float32)
     weights = report_weight[0] * active[None, :]
     weighted = (report_pert[None, :, :] * weights[:, None, :]).astype(jnp.bfloat16)

time: 105 us -> 111 us (1.057)
  the two profiles are of different devices: /device:TPU:0 before, /device:TPU:1 now
where the time goes in v1:
time: 111 us
  blocking collectives  37.6 us (34%)
  matrix products  20.8 us (19%)
  local copies, waits for them, and re-layouts  20.2 us (18%)
  waiting for transfers between devices  14.9 us (13%)
  starting transfers between devices  10.3 us (9%)
  other arithmetic  6.03 us (5%)
  between operations  1.17 us (1%)
    all_gather x1, blocking collectives, per_device(): pieces = lax.all_gather(border, 'region', axis=1, tiled=True)  25.9 us
    psum x1, blocking collectives, per_device(): report_mean = lax.psum(jnp.sum(at_reports, axis=0), 'member') / members  11.7 us
    gather x4, local copies, waits for them, and re-layouts, per_device(): chosen = jnp.take(stacked, chosen_index, axis=0)  8.04 us
    ppermute x2, waiting for transfers between devices, doubled_up(): theirs = lax.ppermute(grown, axis, [(d, d ^ reach) for d in range(ways)])  5.56 us
    dot_general x4, matrix products, make_transform(): root_iter = jnp.einsum('aij,ajk->aik', middle, root_iter, precision=highest)  4.73 us
    dot_general x4, matrix products, make_transform(): jnp.einsum('aij,ajk->aik', root_iter, current, precision=highest)  4.71 us
    ppermute x1, waiting for transfers between devices, extended(): lax.ppermute(lax.slice_in_dim(block, 0, width, axis=dim), axis, backward)  4.4 us
    dot_general x4, matrix products, per_device(): jnp.einsum('kgc,gkj->gcj', anomaly_view, chosen, preferred_element_type=j...  3.83 us
  transfers between devices with their start and end apart: 5, of which 4 were waited for; matrix products, arithmetic and copies ran while one was open for 3% of the time, Pallas kernels for 0%

profile of v1, /device:TPU:1, one launch (start us, length us, event | category | flops | bytes accessed | tf_op | source)
XLA Modules:
  0.0 110.9 jit_solution(5346795213259348145)
XLA Ops:
  1.6 1.2 %copy.24 = bf16[64,2048]{0,1:T(8,128)(2,1)S(1)} copy(bf16[64,2048]{1,0:T(8,128)(2,1)} %param.8) | data formatting | bytes 524288 | tf_op args[0]
  2.8 3.2 %gather_fusion = bf16[1024,64]{1,0:T(8,128)(2,1)S(1)} fusion(bf16[64,2048]{0,1:T(8,128)(2,1)S(1)} %copy.24, s32[1024]{0:T(1024)S(1)} %broadcast_clamp_fusion.1), kind=kCustom, calls=%fused_computation.4 | custom fusion | bytes 266240 | tf_op jit(solution)/shard_map/jit(_take)/gather | solution.py:74
  6.1 25.9 %all_gather.3 = bf16[64,1024]{0,1:T(8,128)(2,1)S(1)} all-gather(bf16[64,128]{0,1:T(8,128)(2,1)S(1)} %slice.37), channel_id=1, replica_groups=mesh['region'=8,'member'=4] {'region'}, dimensions={1}, use_global_device_ids=true | all-gather | bytes 147456 | tf_op jit(solution)/shard_map/all_gather | solution.py:77
  32.1 3.2 %gather_fusion.1 = bf16[1024,64]{1,0:T(8,128)(2,1)S(1)} fusion(bf16[64,1024]{0,1:T(8,128)(2,1)S(1)} %all_gather.3, s32[1024]{0:T(1024)S(1)} %broadcast_clamp_fusion), kind=kCustom, calls=%fused_computation.5 | custom fusion | bytes 266240 | tf_op jit(solution)/shard_map/jit(_take)/gather | solution.py:80
  36.3 11.7 %psum.7 = f32[1024]{0:T(1024)S(1)} all-reduce(f32[1024]{0:T(1024)S(1)} %fusion.51), channel_id=1, replica_groups=mesh['region'=8,'member'=4] {'member'}, use_global_device_ids=true, to_apply=%region_3.4 | all-reduce | flops 1024 | bytes 8192 | tf_op jit(solution)/shard_map/psum | solution.py:83
  48.0 1.2 %fusion.52 = bf16[64,1024]{0,1:T(8,128)(2,1)S(1)} fusion(f32[1024]{0:T(1024)S(1)} %get-tuple-element.18, pred[1024]{0:T(1024)(128)(4,1)S(1)} %get-tuple-element.11, pred[1024]{0:T(1024)(128)(4,1)S(1)} %get-tuple-element.10, bf16[1024,64]{1,0:T(8,128)(2,1)S(1)} %gather_fusion, pred[1024]{0:T(1024)(128)(4,1)S(1)} %get-tuple-element.20, ...), kind=kLoop, calls=%fused_computation.62 | loop fusion | flops 524288 | bytes 401408 | tf_op jit(solution)/shard_map/convert_element_type | solution.py:84
  50.7 3.4 %all-to-all-start = ((bf16[64,4,512]{2,0,1:T(8,128)(2,1)}), bf16[64,4,512]{2,0,1:T(8,128)(2,1)S(1)}, u32[]{:S(2)}, u32[]{:S(2)}) async-start(bf16[64,4,512]{2,0,1:T(8,128)(2,1)} %bitcast.72), calls=%async_computation | async-start | bytes 524288 | tf_op jit(solution)/shard_map/all_to_all | solution.py:98
  55.4 1.5 %collective-permute-start.1 = (bf16[128,1024]{0,1:T(8,128)(2,1)S(1)}, bf16[128,1024]{0,1:T(8,128)(2,1)S(1)}, u32[]{:S(2)}, u32[]{:S(2)}) collective-permute-start(bf16[128,1024]{0,1:T(8,128)(2,1)S(1)} %maximum_select_fusion.1), channel_id=1, source_target_pairs={{0,2},{1,3},{2,0},{3,1},{4,6},{5,7},{6,4},{7,5},{8,10},{9,11},{10,... | collective-permute-start | bytes 786440 | tf_op jit(solution)/shard_map/ppermute | solution.py:15
  57.2 2.0 %all-to-all-done = bf16[64,4,512]{2,0,1:T(8,128)(2,1)S(1)} async-done(((bf16[64,4,512]{2,0,1:T(8,128)(2,1)}), bf16[64,4,512]{2,0,1:T(8,128)(2,1)S(1)}, u32[]{:S(2)}, u32[]{:S(2)}) %all-to-all-start) | async-done | bytes 262176 | tf_op jit(solution)/shard_map/all_to_all | solution.py:98
  59.3 5.6 %collective-permute-done.1 = bf16[128,1024]{0,1:T(8,128)(2,1)S(1)} collective-permute-done((bf16[128,1024]{0,1:T(8,128)(2,1)S(1)}, bf16[128,1024]{0,1:T(8,128)(2,1)S(1)}, u32[]{:S(2)}, u32[]{:S(2)}) %collective-permute-start.1) | collective-permute-done | bytes 262176 | tf_op jit(solution)/shard_map/ppermute | solution.py:15
  66.1 1.9 %multiply_reduce_fusion = (f32[4]{0:T(128)S(1)}, f32[4,256,256]{2,1,0:T(8,128)S(1)}) fusion(bf16[128,1024]{0,1:T(8,128)(2,1)S(1)} %maximum_select_fusion.1, bf16[128,1024]{0,1:T(8,128)(2,1)} %copy-done.4, pred[]{:T(512)S(6)} %eq.59, f32[4,1024]{1,0:T(4,128)S(1)} %bitcast_multiply_fusion, f32[256,1024]{1,0:T(8,128)S(1)} %copy.26, f32[256,256]{1,0:T(8,128)S(1)} %fusion.53), kind=kOutput, calls=%fused_computation.46 | convolution fusion | flops 542113792 | bytes 2899985 | tf_op jit(solution)/shard_map/ako,jo->akj/dot_general | solution.py:90
  68.0 1.2 %fusion.19 = f32[4,256,256]{2,1,0:T(8,128)S(1)} fusion(f32[256,256]{1,0:T(8,128)S(1)} %fusion.54, f32[256,256]{1,0:T(8,128)S(1)} %fusion.55, f32[4,256,256]{2,1,0:T(8,128)S(1)} %get-tuple-element.24, f32[4]{0:T(128)S(1)} %get-tuple-element.22), kind=kOutput, calls=%fused_computation.32 | convolution fusion | flops 806092800 | bytes 2621456 | tf_op jit(solution)/shard_map/aij,ajk->aik/dot_general | solution.py:43
  69.2 1.2 %fusion.56 = f32[4,256,256]{2,1,0:T(8,128)S(1)} fusion(f32[4,256,256]{2,1,0:T(8,128)S(1)} %fusion.19, f32[4,256,256]{2,1,0:T(8,128)S(1)} %get-tuple-element.24, f32[4]{0:T(128)S(1)} %get-tuple-element.22), kind=kOutput, calls=%fused_computation.71 | convolution fusion | flops 805568512 | bytes 3145744 | tf_op jit(solution)/shard_map/aij,ajk->aik/dot_general | solution.py:46
  70.4 1.1 fusion.48
  71.5 1.2 %fusion.18 = f32[4,256,256]{2,1,0:T(8,128)S(1)} fusion(f32[4,256,256]{2,1,0:T(8,128)S(1)} %fusion.48, f32[4,256,256]{2,1,0:T(8,128)S(1)} %fusion.56, f32[256,256]{1,0:T(8,128)S(1)} %fusion.55), kind=kOutput, calls=%fused_computation.30 | convolution fusion | flops 805830656 | bytes 3407872 | tf_op jit(solution)/shard_map/aij,ajk->aik/dot_general | solution.py:43
  72.7 1.1 %fusion.80 = f32[4,256,256]{2,1,0:T(8,128)S(1)} fusion(f32[4,256,256]{2,1,0:T(8,128)S(1)} %fusion.56, f32[4,256,256]{2,1,0:T(8,128)S(1)} %fusion.18), kind=kOutput, calls=%fused_computation.161 | convolution fusion | flops 805306368 | bytes 3145728 | tf_op jit(solution)/shard_map/aij,ajk->aik/dot_general | solution.py:46
  73.8 1.1 %fusion.79 = f32[4,256,256]{2,1,0:T(8,128)S(1)} fusion(f32[4,256,256]{2,1,0:T(8,128)S(1)} %fusion.18, f32[4,256,256]{2,1,0:T(8,128)S(1)} %fusion.48), kind=kOutput, calls=%fused_computation.160 | convolution fusion | flops 805306368 | bytes 3145728 | tf_op jit(solution)/shard_map/aij,ajk->aik/dot_general | solution.py:47
  75.0 1.2 %fusion.17 = f32[4,256,256]{2,1,0:T(8,128)S(1)} fusion(f32[4,256,256]{2,1,0:T(8,128)S(1)} %fusion.79, f32[4,256,256]{2,1,0:T(8,128)S(1)} %fusion.80, f32[256,256]{1,0:T(8,128)S(1)} %fusion.55), kind=kOutput, calls=%fused_computation.28 | convolution fusion | flops 805830656 | bytes 3407872 | tf_op jit(solution)/shard_map/aij,ajk->aik/dot_general | solution.py:43
  76.2 1.1 %fusion.82 = f32[4,256,256]{2,1,0:T(8,128)S(1)} fusion(f32[4,256,256]{2,1,0:T(8,128)S(1)} %fusion.80, f32[4,256,256]{2,1,0:T(8,128)S(1)} %fusion.17), kind=kOutput, calls=%fused_computation.163 | convolution fusion | flops 805306368 | bytes 3145728 | tf_op jit(solution)/shard_map/aij,ajk->aik/dot_general | solution.py:46
  77.3 1.4 %fusion.81 = f32[4,256,256]{2,1,0:T(8,128)S(1)} fusion(f32[4,256,256]{2,1,0:T(8,128)S(1)} %fusion.17, f32[4,256,256]{2,1,0:T(8,128)S(1)} %fusion.79), kind=kOutput, calls=%fused_computation.162 | convolution fusion | flops 805306368 | bytes 3145728 | tf_op jit(solution)/shard_map/aij,ajk->aik/dot_general | solution.py:47
  78.7 1.2 %fusion.16 = f32[4,256,256]{2,1,0:T(8,128)S(1)} fusion(f32[4,256,256]{2,1,0:T(8,128)S(1)} %fusion.81, f32[4,256,256]{2,1,0:T(8,128)S(1)} %fusion.82, f32[256,256]{1,0:T(8,128)S(1)} %fusion.55), kind=kOutput, calls=%fused_computation.26 | convolution fusion | flops 805830656 | bytes 3407872 | tf_op jit(solution)/shard_map/aij,ajk->aik/dot_general | solution.py:43
  79.9 1.1 %convolution_divide_fusion = f32[4,256,256]{2,1,0:T(8,128)S(1)} fusion(f32[4,256,256]{2,1,0:T(8,128)S(1)} %fusion.16, f32[4,256,256]{2,1,0:T(8,128)S(1)} %fusion.81, f32[4]{0:T(128)S(1)} %get-tuple-element.21), kind=kOutput, calls=%fused_computation.24 | convolution fusion | flops 805568512 | bytes 3145744 | tf_op jit(solution)/shard_map/aij,ajk->aik/dot_general | solution.py:47
  83.5 2.7 %collective-permute-start.2 = (bf16[1,4,256,256]{3,2,1,0:T(8,128)(2,1)S(1)}, bf16[1,4,256,256]{3,2,1,0:T(8,128)(2,1)S(1)}, u32[]{:S(2)}, u32[]{:S(2)}) collective-permute-start(bf16[1,4,256,256]{3,2,1,0:T(8,128)(2,1)S(1)} %fusion.45), channel_id=1, source_target_pairs={{0,1},{1,2},{2,3},{4,5},{5,6},{6,7},{8,9},{9,10},{10,11},{12,13},{... | collective-permute-start | bytes 1572872 | tf_op jit(solution)/shard_map/ppermute | solution.py:28
  86.2 1.9 %collective-permute-start.3 = (bf16[1,4,256,256]{3,2,1,0:T(8,128)(2,1)S(1)}, bf16[1,4,256,256]{3,2,1,0:T(8,128)(2,1)S(1)}, u32[]{:S(2)}, u32[]{:S(2)}) collective-permute-start(bf16[1,4,256,256]{3,2,1,0:T(8,128)(2,1)S(1)} %fusion.45), channel_id=1, source_target_pairs={{1,0},{2,1},{3,2},{5,4},{6,5},{7,6},{9,8},{10,9},{11,10},{13,12},{... | collective-permute-start | bytes 1572872 | tf_op jit(solution)/shard_map/ppermute | solution.py:31
  89.4 2.9 %collective-permute-done.2 = bf16[1,4,256,256]{3,2,1,0:T(8,128)(2,1)S(1)} collective-permute-done((bf16[1,4,256,256]{3,2,1,0:T(8,128)(2,1)S(1)}, bf16[1,4,256,256]{3,2,1,0:T(8,128)(2,1)S(1)}, u32[]{:S(2)}, u32[]{:S(2)}) %collective-permute-start.2) | collective-permute-done | bytes 524320 | tf_op jit(solution)/shard_map/ppermute | solution.py:28
  92.3 4.4 %collective-permute-done.3 = bf16[1,4,256,256]{3,2,1,0:T(8,128)(2,1)S(1)} collective-permute-done((bf16[1,4,256,256]{3,2,1,0:T(8,128)(2,1)S(1)}, bf16[1,4,256,256]{3,2,1,0:T(8,128)(2,1)S(1)}, u32[]{:S(2)}, u32[]{:S(2)}) %collective-permute-start.3) | collective-permute-done | bytes 524320 | tf_op jit(solution)/shard_map/ppermute | solution.py:31
  96.9 2.0 %gather_fusion.3 = bf16[16,256,256]{2,1,0:T(8,128)(2,1)} fusion(bf16[12,256,256]{2,1,0:T(8,128)(2,1)S(1)} %bitcast.76, s32[1024]{0:T(1024)S(1)} %pad_clamp_fusion.2), kind=kCustom, calls=%fused_computation.1.clone | custom fusion | bytes 4194368 | tf_op jit(solution)/shard_map/jit(_take)/gather | solution.py:111
  98.9 2.0 %gather_fusion.4 = bf16[16,256,256]{2,1,0:T(8,128)(2,1)} fusion(bf16[12,256,256]{2,1,0:T(8,128)(2,1)S(1)} %bitcast.77, s32[1024]{0:T(1024)S(1)} %pad_clamp_fusion.1), kind=kCustom, calls=%fused_computation.2.clone | custom fusion | bytes 4194368 | tf_op jit(solution)/shard_map/jit(_take)/gather | solution.py:111
  100.8 2.0 %gather_fusion.5 = bf16[16,256,256]{2,1,0:T(8,128)(2,1)} fusion(bf16[12,256,256]{2,1,0:T(8,128)(2,1)S(1)} %bitcast.78, s32[1024]{0:T(1024)S(1)} %pad_clamp_fusion), kind=kCustom, calls=%fused_computation.3.clone | custom fusion | bytes 4194368 | tf_op jit(solution)/shard_map/jit(_take)/gather | solution.py:111
  102.9 2.0 %gather_fusion.2 = bf16[16,256,256]{2,1,0:T(8,128)(2,1)} fusion(bf16[12,256,256]{2,1,0:T(8,128)(2,1)S(1)} %bitcast.79, s32[1024]{0:T(1024)S(1)} %pad_clamp_fusion.3), kind=kCustom, calls=%fused_computation.clone | custom fusion | bytes 4194368 | tf_op jit(solution)/shard_map/jit(_take)/gather | solution.py:111
  104.9 2.3 %fusion.29 = f32[16,32,256]{2,1,0:T(8,128)S(1)} fusion(bf16[256,16,32]{0,2,1:T(8,128)(2,1)S(1)} %subtract_convert_fusion.1, bf16[16,256,256]{2,1,0:T(8,128)(2,1)} %gather_fusion.3, pred[16]{0:T(512)(128)(4,1)S(1)} %compare_and_fusion.4, f32[16,32]{1,0:T(8,128)S(1)} %mul.175), kind=kOutput, calls=%fused_computation.36 | convolution fusion | flops 68288512 | bytes 2885648 | tf_op jit(solution)/shard_map/kgc,gkj->gcj/dot_general | solution.py:112
  107.7 1.0 copy-done.1
  (75 shorter events, 12.7 us)
Async XLA Ops:
  0.0 6.0 %copy-start.6 = (s32[1,1024]{1,0:T(1,128)S(1)}, s32[1,1024]{1,0:T(1,128)}, u32[]{:S(2)}) copy-start(s32[1,1024]{1,0:T(1,128)} %param.11) | copy-start | bytes 12292
  0.0 48.0 %copy-start.9 = (f32[1,1024]{1,0:T(1,128)S(1)}, f32[1,1024]{1,0:T(1,128)}, u32[]{:S(2)}) copy-start(f32[1,1024]{1,0:T(1,128)} %param.9) | copy-start | bytes 12292
  2.8 47.2 %copy-start.3 = (bf16[64,2048]{1,0:T(8,128)(2,1)S(1)}, bf16[64,2048]{1,0:T(8,128)(2,1)}, u32[]{:S(2)}) copy-start(bf16[64,2048]{1,0:T(8,128)(2,1)} %param.8) | copy-start | bytes 786436
  6.1 48.8 %copy-start.7 = (f32[4,512]{1,0:T(4,128)S(1)}, f32[4,512]{1,0:T(4,128)}, u32[]{:S(2)}) copy-start(f32[4,512]{1,0:T(4,128)} %param.13) | copy-start | bytes 24580
  6.1 48.9 %copy-start.8 = (f32[1,4,1024]{2,1,0:T(4,128)S(1)}, f32[1,4,1024]{2,1,0:T(4,128)}, u32[]{:S(2)}) copy-start(f32[1,4,1024]{2,1,0:T(4,128)} %param.12) | copy-start | bytes 49156
  49.2 5.8 %collective-permute-start = (bf16[64,1024]{0,1:T(8,128)(2,1)S(1)}, bf16[64,1024]{0,1:T(8,128)(2,1)S(1)}, u32[]{:S(2)}, u32[]{:S(2)}) collective-permute-start(bf16[64,1024]{0,1:T(8,128)(2,1)S(1)} %fusion.52), channel_id=1, source_target_pairs={{0,1},{1,0},{2,3},{3,2},{4,5},{5,4},{6,7},{7,6},{8,9},{9,8},{10,11... | collective-permute-start | bytes 393224 | tf_op jit(solution)/shard_map/ppermute | solution.py:15
  50.7 8.6 %all-to-all-start = ((bf16[64,4,512]{2,0,1:T(8,128)(2,1)}), bf16[64,4,512]{2,0,1:T(8,128)(2,1)S(1)}, u32[]{:S(2)}, u32[]{:S(2)}) async-start(bf16[64,4,512]{2,0,1:T(8,128)(2,1)} %bitcast.72), calls=%async_computation | async-start | bytes 524288 | tf_op jit(solution)/shard_map/all_to_all | solution.py:98
  55.4 9.5 %collective-permute-start.1 = (bf16[128,1024]{0,1:T(8,128)(2,1)S(1)}, bf16[128,1024]{0,1:T(8,128)(2,1)S(1)}, u32[]{:S(2)}, u32[]{:S(2)}) collective-permute-start(bf16[128,1024]{0,1:T(8,128)(2,1)S(1)} %maximum_select_fusion.1), channel_id=1, source_target_pairs={{0,2},{1,3},{2,0},{3,1},{4,6},{5,7},{6,4},{7,5},{8,10},{9,11},{10,... | collective-permute-start | bytes 786440 | tf_op jit(solution)/shard_map/ppermute | solution.py:15
  64.9 0.7 copy-start.4
  79.9 1.2 %copy-start.5 = (bf16[128,1024]{0,1:T(8,128)(2,1)S(1)}, bf16[128,1024]{0,1:T(8,128)(2,1)}, u32[]{:S(2)}) copy-start(bf16[128,1024]{0,1:T(8,128)(2,1)} %copy-done.4) | copy-start | bytes 786436
  83.5 8.8 %collective-permute-start.2 = (bf16[1,4,256,256]{3,2,1,0:T(8,128)(2,1)S(1)}, bf16[1,4,256,256]{3,2,1,0:T(8,128)(2,1)S(1)}, u32[]{:S(2)}, u32[]{:S(2)}) collective-permute-start(bf16[1,4,256,256]{3,2,1,0:T(8,128)(2,1)S(1)} %fusion.45), channel_id=1, source_target_pairs={{0,1},{1,2},{2,3},{4,5},{5,6},{6,7},{8,9},{9,10},{10,11},{12,13},{... | collective-permute-start | bytes 1572872 | tf_op jit(solution)/shard_map/ppermute | solution.py:28
  86.2 10.5 %collective-permute-start.3 = (bf16[1,4,256,256]{3,2,1,0:T(8,128)(2,1)S(1)}, bf16[1,4,256,256]{3,2,1,0:T(8,128)(2,1)S(1)}, u32[]{:S(2)}, u32[]{:S(2)}) collective-permute-start(bf16[1,4,256,256]{3,2,1,0:T(8,128)(2,1)S(1)} %fusion.45), channel_id=1, source_target_pairs={{1,0},{2,1},{3,2},{5,4},{6,5},{7,6},{9,8},{10,9},{11,10},{13,12},{... | collective-permute-start | bytes 1572872 | tf_op jit(solution)/shard_map/ppermute | solution.py:31
  104.9 2.3 %copy-start.2 = (bf16[16,256,256]{2,1,0:T(8,128)(2,1)S(1)}, bf16[16,256,256]{2,1,0:T(8,128)(2,1)}, u32[]{:S(2)}) copy-start(bf16[16,256,256]{2,1,0:T(8,128)(2,1)} %gather_fusion.4) | copy-start | bytes 6291460
  107.2 1.6 %copy-start.1 = (bf16[16,256,256]{2,1,0:T(8,128)(2,1)S(1)}, bf16[16,256,256]{2,1,0:T(8,128)(2,1)}, u32[]{:S(2)}) copy-start(bf16[16,256,256]{2,1,0:T(8,128)(2,1)} %gather_fusion.5) | copy-start | bytes 6291460
  107.7 1.8 %copy-start = (bf16[16,256,256]{2,1,0:T(8,128)(2,1)S(1)}, bf16[16,256,256]{2,1,0:T(8,128)(2,1)}, u32[]{:S(2)}) copy-start(bf16[16,256,256]{2,1,0:T(8,128)(2,1)} %gather_fusion.2) | copy-start | bytes 6291460
